TPU v7x, 512 devices: a whole 4x8x8 slice. The times are simulated.
512 devices in a mesh: stu: 16 (over z_lo, x), que: 32 (over z_hi, y, core).
Axes of the slice: x: 4, y: 8, z: 8 (z_hi: 2, z_lo: 4; z = z_hi * 4 + z_lo), core: 2. Of those that a mesh axis runs over, the one named last changes fastest.
Arguments:
- codes: int32 [4096, 4096], P('stu', 'que'), may hold values from 0 to 2
- theta: float32 [4096, 64], P(('stu', 'que')), may hold values from -6 to 6
- disc: float32 [4096, 64], P(('que', 'stu')), may hold values from -0.75 to 0.75
- intercept: float32 [4096], P(('que', 'stu')), may hold values from -5 to 5
Outputs:
- step_abilities: float32 [4096, 64], P(('stu', 'que'))
- step_disc: float32 [4096, 64], P(('que', 'stu'))
- step_intercept: float32 [4096], P(('que', 'stu'))
All inputs are finite; a program needn't handle non-finite values.
Results may differ from a plain program's by a relative error of at most 0.0003.
Values sent between devices are 32-bit elements; how exact they have to be, the bound alone decides.
A program may use at most 64 MiB of HBM per device.

v0:
```python
import jax
import jax.numpy as jnp
from jax import lax
from jax.sharding import PartitionSpec as P

ITERS = 2
HIGH = lax.Precision.HIGHEST


def matmul(left, right):
    return jnp.dot(left, right, precision=HIGH, preferred_element_type=jnp.float32)


def contract_rows(left, right):
    return lax.dot_general(
        left, right, (((0,), (0,)), ((), ())), precision=HIGH, preferred_element_type=jnp.float32
    )


def local_inner(left, right):
    return jnp.sum(left[0] * right[0]) + jnp.sum(left[1] * right[1]) + jnp.sum(left[2] * right[2])


def squared(residual, precond):
    return lax.psum(local_inner(residual, precond), ("stu", "que"))


def combine(first, factor, second):
    return jax.tree.map(lambda u, v: u + factor * v, first, second)


def shards(codes, theta, disc, intercept):
    theta_rows = lax.all_gather(theta, "que", axis=0, tiled=True)
    disc_cols, icpt_cols = (
        lax.all_gather(disc, "stu", axis=0, tiled=True),
        lax.all_gather(intercept, "stu", axis=0, tiled=True),
    )
    logit = matmul(theta_rows, disc_cols.T) + icpt_cols[None, :]
    prob = jax.nn.sigmoid(logit)
    observed = (codes > 0).astype(jnp.float32)
    correct = (codes == 2).astype(jnp.float32)
    resid = observed * (prob - correct)
    weight = observed * prob * (1.0 - prob)
    row_one = matmul(resid, disc_cols)
    row_two = matmul(weight, disc_cols * disc_cols)
    col_one = contract_rows(resid, theta_rows)
    col_two = contract_rows(weight, theta_rows * theta_rows)
    col_three = jnp.sum(resid, 0)
    col_four = jnp.sum(weight, 0)
    row_sum = (
        lax.psum_scatter(row_one, "que", scatter_dimension=0, tiled=True),
        lax.psum_scatter(row_two, "que", scatter_dimension=0, tiled=True),
    )
    col_sum = (
        lax.psum_scatter(col_one, "stu", scatter_dimension=0, tiled=True),
        lax.psum_scatter(col_two, "stu", scatter_dimension=0, tiled=True),
        lax.psum_scatter(col_three, "stu", scatter_dimension=0, tiled=True),
        lax.psum_scatter(col_four, "stu", scatter_dimension=0, tiled=True),
    )
    own = (theta, disc, intercept)
    grad = (row_sum[0] + own[0], col_sum[0] + own[1], col_sum[2] + own[2])
    diag = (row_sum[1] + 1.0, col_sum[1] + 1.0, col_sum[3] + 1.0)
    solution = jax.tree.map(jnp.zeros_like, grad)
    residual = jax.tree.map(lambda u: -u, grad)
    precond = jax.tree.map(lambda u, d: u / d, residual, diag)
    direction = precond
    norm_now = squared(residual, precond)
    for step in range(ITERS):
        vt_rows = lax.all_gather(direction[0], "que", axis=0, tiled=True)
        va_cols = lax.all_gather(direction[1], "stu", axis=0, tiled=True)
        vb_cols = lax.all_gather(direction[2], "stu", axis=0, tiled=True)
        left = jnp.concatenate([vt_rows, theta_rows], 1)
        right = jnp.concatenate([disc_cols, va_cols], 1)
        change = matmul(left, right.T) + vb_cols[None, :]
        scaled = weight * change
        part_rows = matmul(scaled, disc_cols)
        part_disc = contract_rows(scaled, theta_rows)
        part_icpt = jnp.sum(scaled, 0)
        summed_rows = lax.psum_scatter(part_rows, "que", scatter_dimension=0, tiled=True)
        summed_disc = lax.psum_scatter(part_disc, "stu", scatter_dimension=0, tiled=True)
        summed_icpt = lax.psum_scatter(part_icpt, "stu", scatter_dimension=0, tiled=True)
        image = (summed_rows + direction[0], summed_disc + direction[1], summed_icpt + direction[2])
        alpha = norm_now / lax.psum(local_inner(direction, image), ("stu", "que"))
        solution = combine(solution, alpha, direction)
        residual = combine(residual, -alpha, image)
        if step + 1 < ITERS:
            precond = jax.tree.map(lambda u, d: u / d, residual, diag)
            norm_next = squared(residual, precond)
            ratio = norm_next / norm_now
            direction = combine(precond, ratio, direction)
            norm_now = norm_next
    result = jax.tree.map(lambda u, d: u * jnp.sqrt(d), solution, diag)
    return (result[0], result[1], result[2])


def solution(mesh):
    placed = (P("stu", "que"), P(("stu", "que"), None), P(("que", "stu"), None), P(("que", "stu")))
    return jax.shard_map(
        shards,
        mesh=mesh,
        in_specs=placed,
        out_specs=(P(("stu", "que"), None), P(("que", "stu"), None), P(("que", "stu"))),
        check_vma=False,
    )
```

profile of v0, /device:TPU:1, one launch (start us, length us, event | category | flops | bytes accessed | tf_op | source)
XLA Modules:
  0.0 1810.6 jit_solution(3583325412611648461)
XLA Ops:
  7.2 60.0 %all_gather.27 = f32[256,64]{1,0:T(8,128)S(1)} all-gather(f32[8,64]{1,0:T(8,128)} %param.5), channel_id=1, replica_groups=mesh['stu'=16,'que'=32] {'que'}, dimensions={0}, use_global_device_ids=true | all-gather | bytes 67584 | tf_op jit(solution)/shard_map/all_gather | solution.py:33
  67.2 0.7 copy-done.5
  67.9 0.6 fusion.47
  69.4 36.2 %all-reduce = f32[128]{0:T(128)S(1)} all-reduce(f32[128]{0:T(128)S(1)} %dynamic-update-slice), channel_id=1, replica_groups=mesh['stu'=16,'que'=32] {'stu'}, use_global_device_ids=true, to_apply=%add | all-reduce | flops 128 | bytes 1024
  105.6 30.4 %all_gather.28 = f32[128,64]{1,0:T(8,128)S(1)} all-gather(f32[8,64]{1,0:T(8,128)S(1)} %copy-done.1), channel_id=1, replica_groups=mesh['stu'=16,'que'=32] {'stu'}, dimensions={0}, use_global_device_ids=true | all-gather | bytes 34816 | tf_op jit(solution)/shard_map/all_gather | solution.py:35
  136.4 1.0 fusion.37
  137.4 1.0 fusion.10
  138.4 32.3 %all-reduce.20 = (f32[128]{0:T(128)S(1)}, f32[128]{0:T(128)S(1)}) all-reduce(f32[128]{0:T(128)S(1)} %get-tuple-element.35, f32[128]{0:T(128)S(1)} %get-tuple-element.31), channel_id=6, replica_groups=mesh['stu'=16,'que'=32] {'stu'}, use_global_device_ids=true, to_apply=%region_7.0.clone | all-reduce | flops 256 | bytes 2048
  171.5 0.5 copy-done.4
  172.1 0.9 fusion.38
  173.0 0.9 fusion.18
  174.0 1.3 dynamic-slice.3
  176.0 152.3 %all-reduce.32.cloned.1.call-done = (f32[128,64]{1,0:T(8,128)}, f32[128,64]{1,0:T(8,128)}, f32[128]{0:T(128)}) async-done(((f32[128,64]{1,0:T(8,128)}, f32[128,64]{1,0:T(8,128)}, f32[128]{0:T(128)}), (f32[128,64]{1,0:T(8,128)}, f32[128,64]{1,0:T(8,128)}, f32[128]{0:T(128)})) %all-reduce.32.cloned.1.call-update) | async-done | bytes 66064
  328.2 0.7 fusion.29
  328.9 35.5 %all_gather.31 = f32[128,64]{1,0:T(8,128)S(1)} all-gather(f32[8,64]{1,0:T(8,128)S(1)} %get-tuple-element.26), channel_id=1, replica_groups=mesh['stu'=16,'que'=32] {'stu'}, dimensions={0}, use_global_device_ids=true | all-gather | bytes 34816 | tf_op jit(solution)/shard_map/all_gather | solution.py:70
  364.4 318.1 %all-reduce.30.cloned.1.call-done = (f32[256,64]{1,0:T(8,128)}, f32[256,64]{1,0:T(8,128)}) async-done(((f32[256,64]{1,0:T(8,128)}, f32[256,64]{1,0:T(8,128)}), (f32[256,64]{1,0:T(8,128)}, f32[256,64]{1,0:T(8,128)})) %all-reduce.30.cloned.1.call-update) | async-done | bytes 131088
  682.5 0.7 fusion.27
  683.2 47.3 %all_gather.30 = f32[256,64]{1,0:T(8,128)S(1)} all-gather(f32[8,64]{1,0:T(8,128)S(1)} %get-tuple-element.33), channel_id=1, replica_groups=mesh['stu'=16,'que'=32] {'que'}, dimensions={0}, use_global_device_ids=true | all-gather | bytes 67584 | tf_op jit(solution)/shard_map/all_gather | solution.py:69
  730.5 0.7 copy-done.3
  731.2 0.4 fusion.48
  731.6 0.9 fusion.50
  732.5 0.4 fusion.51
  733.0 67.3 %all-reduce.18 = (f32[128,64]{1,0:T(8,128)S(1)}, f32[128]{0:T(128)S(1)}) all-reduce(f32[128,64]{1,0:T(8,128)S(1)} %fusion.51, f32[128]{0:T(128)S(1)} %get-tuple-element.39), channel_id=9, replica_groups=mesh['stu'=16,'que'=32] {'stu'}, use_global_device_ids=true, to_apply=%region_14.0.clone | all-reduce | flops 8320 | bytes 66560
  800.3 0.7 multiply_reduce_fusion.2
  800.9 0.8 multiply_reduce_fusion.7
  801.7 247.6 %all-reduce.26.cloned.1.call-done = f32[256,64]{1,0:T(8,128)} async-done(((f32[256,64]{1,0:T(8,128)}), f32[256,64]{1,0:T(8,128)}) %all-reduce.26.cloned.1.call-update) | async-done | bytes 65552
  1049.3 1.3 multiply_reduce_fusion.3
  1054.4 98.3 %all-reduce.15 = (f32[]{:T(128)}, f32[]{:T(128)}) all-reduce(f32[]{:T(128)S(6)} %add.156, f32[]{:T(128)S(6)} %add.163), channel_id=1, replica_groups=mesh['stu'=16,'que'=32] {'stu','que'}, use_global_device_ids=true, to_apply=%region_11.0 | all-reduce | flops 2 | bytes 16 | tf_op jit(solution)/shard_map/psum | solution.py:25
  1154.1 1.4 multiply_reduce_fusion
  1155.4 0.7 multiply_reduce_fusion.6
  1156.1 1.3 multiply_reduce_fusion.1
  1159.3 94.4 %psum.30 = f32[]{:T(128)} all-reduce(f32[]{:T(128)S(6)} %add.168), channel_id=1, replica_groups=mesh['stu'=16,'que'=32] {'stu','que'}, use_global_device_ids=true, to_apply=%region_23.0 | all-reduce | flops 1 | bytes 8 | tf_op jit(solution)/shard_map/psum | solution.py:25
  1255.1 0.7 multiply_add_fusion
  1255.8 34.9 %all-reduce.2 = f32[128]{0:T(128)S(1)} all-reduce(f32[128]{0:T(128)S(1)} %get-tuple-element.22), channel_id=1, replica_groups=mesh['stu'=16,'que'=32] {'stu'}, use_global_device_ids=true, to_apply=%add.2 | all-reduce | flops 128 | bytes 1024
  1290.8 30.4 %all_gather.34 = f32[128,64]{1,0:T(8,128)S(1)} all-gather(f32[8,64]{1,0:T(8,128)S(1)} %multiply_add_fusion), channel_id=1, replica_groups=mesh['stu'=16,'que'=32] {'stu'}, dimensions={0}, use_global_device_ids=true | all-gather | bytes 34816 | tf_op jit(solution)/shard_map/all_gather | solution.py:70
  1321.2 0.7 multiply_add_fusion.1
  1321.9 63.4 %all_gather.33 = f32[256,64]{1,0:T(8,128)S(1)} all-gather(f32[8,64]{1,0:T(8,128)S(1)} %multiply_add_fusion.1), channel_id=1, replica_groups=mesh['stu'=16,'que'=32] {'que'}, dimensions={0}, use_global_device_ids=true | all-gather | bytes 67584 | tf_op jit(solution)/shard_map/all_gather | solution.py:69
  1385.2 0.4 fusion.49
  1385.6 0.9 fusion.52
  1386.5 0.4 fusion.53
  1387.0 64.5 %all-reduce.17 = (f32[128,64]{1,0:T(8,128)S(1)}, f32[128]{0:T(128)S(1)}) all-reduce(f32[128,64]{1,0:T(8,128)S(1)} %fusion.53, f32[128]{0:T(128)S(1)} %get-tuple-element.41), channel_id=12, replica_groups=mesh['stu'=16,'que'=32] {'stu'}, use_global_device_ids=true, to_apply=%region_26.0.clone | all-reduce | flops 8320 | bytes 66560
  1451.5 0.6 fusion.23
  1452.1 0.7 fusion.30
  1452.8 246.5 %all-reduce.28.cloned.1.call-done = f32[256,64]{1,0:T(8,128)} async-done(((f32[256,64]{1,0:T(8,128)}), f32[256,64]{1,0:T(8,128)}) %all-reduce.28.cloned.1.call-update) | async-done | bytes 65552
  1699.3 1.3 fusion.22
  1702.5 98.3 %psum.31 = f32[]{:T(128)} all-reduce(f32[]{:T(128)S(6)} %add.178), channel_id=1, replica_groups=mesh['stu'=16,'que'=32] {'stu','que'}, use_global_device_ids=true, to_apply=%region_31.0 | all-reduce | flops 1 | bytes 8 | tf_op jit(solution)/shard_map/psum | solution.py:83
  1802.2 1.3 sqrt_multiply_fusion
  1803.5 0.6 sqrt_multiply_fusion.2
  (26 shorter events, 1.1 us)
Async XLA Ops:
  7.2 128.9 %copy-start = (s32[256,128]{1,0:T(8,128)S(1)}, s32[256,128]{1,0:T(8,128)}, u32[]{:S(2)}) copy-start(s32[256,128]{1,0:T(8,128)} %param.4) | copy-start | bytes 393220
  7.2 321.0 %all-reduce.32.cloned.1.call-start = ((), (), s32[]{:S(2)}) async-start(), calls=%async_computation.3 | async-start | bytes 263168
  67.2 0.7 copy-start.5
  68.5 0.7 copy-start.6
  69.2 36.4 %copy-start.1 = (f32[8,64]{1,0:T(8,128)S(1)}, f32[8,64]{1,0:T(8,128)}, u32[]{:S(2)}) copy-start(f32[8,64]{1,0:T(8,128)} %param.6) | copy-start | bytes 6148
  171.5 0.5 copy-start.4
  172.1 510.4 %all-reduce.30.cloned.1.call-start = ((), (), s32[]{:S(2)}) async-start(), calls=%async_computation.2 | async-start | bytes 524288
  174.0 875.3 %all-reduce.26.cloned.1.call-start = ((), (), s32[]{:S(2)}) async-start(), calls=%async_computation | async-start | bytes 262144
  328.9 353.6 %copy-start.2 = (f32[8,64]{1,0:T(8,128)S(1)}, f32[8,64]{1,0:T(8,128)}, u32[]{:S(2)}) copy-start(f32[8,64]{1,0:T(8,128)} %param.5) | copy-start | bytes 6148
  730.5 0.7 copy-start.3
  732.9 966.4 %all-reduce.28.cloned.1.call-start = ((), (), s32[]{:S(2)}) async-start(), calls=%async_computation.1 | async-start | bytes 262144
Sparse Core Ops, SparseCore 0:
  172.2 155.9 all-reduce.31
  331.1 351.3 all-reduce.29
  733.0 316.2 all-reduce.25
  1387.1 312.2 all-reduce.27
where the time goes:
time: 1810 us
  waiting for transfers between devices  965 us (53%)
  blocking collectives  793 us (44%)
  between operations  27.5 us (2%)
    unnamed x8, waiting for transfers between devices  965 us
    unnamed x5, blocking collectives  235 us
    psum x2, blocking collectives, squared(): return lax.psum(local_inner(residual, precond), ('stu', 'que'))  193 us
    all_gather x2, blocking collectives, shards(): vt_rows = lax.all_gather(direction[0], 'que', axis=0, tiled=True)  111 us
    psum x1, blocking collectives, shards(): alpha = norm_now / lax.psum(local_inner(direction, image), ('stu', 'que'))  98.3 us
    all_gather x2, blocking collectives, shards(): va_cols = lax.all_gather(direction[1], 'stu', axis=0, tiled=True)  65.9 us
    all_gather x1, blocking collectives, shards(): theta_rows = lax.all_gather(theta, 'que', axis=0, tiled=True)  60 us
  transfers between devices with their start and end apart: 4, of which 4 were waited for; matrix products, arithmetic and copies ran while one was open for 0% of the time, Pallas kernels for 0%

commit v1 on v0

--- a/solution.py
+++ b/solution.py
@@ -66,7 +66,9 @@
     direction = precond
     norm_now = squared(residual, precond)
     for step in range(ITERS):
-        vt_rows = lax.all_gather(direction[0], "que", axis=0, tiled=True)
+        block = direction[0]
+        stack = jnp.stack([block] * lax.axis_size("que"))
+        vt_rows = jnp.concatenate(lax.all_to_all(stack, "que", 0, 0), axis=0)
         va_cols = lax.all_gather(direction[1], "stu", axis=0, tiled=True)
         vb_cols = lax.all_gather(direction[2], "stu", axis=0, tiled=True)
         left = jnp.concatenate([vt_rows, theta_rows], 1)

time: 1810 us -> 1740 us (0.961)
  blocking collectives: 793 us -> 675 us
  starting transfers between devices: 0.16 us -> 18.9 us
    all_gather x2 -> x0, blocking collectives: 111 us -> none  [shards(): vt_rows = lax.all_gather(direction[0], 'que', axis=0, tiled=True)]
    unnamed x8, waiting for transfers between devices: 965 us -> 983 us
    all_to_all x0 -> x2, starting transfers between devices: none -> 18.7 us  [shards(): vt_rows = jnp.concatenate(lax.all_to_all(stack, 'que', 0, 0), axis=0)]
  transfers between devices with their start and end apart: 4 -> 6, of which waited for: 4 -> 4; matrix products, arithmetic and copies ran while one was open for 0% -> 0% of each run, Pallas kernels for 0% -> 0%
where the time goes in v1:
time: 1740 us; the launch traced here: 1730 us
  waiting for transfers between devices  983 us (56%)
  blocking collectives  675 us (39%)
  between operations  27.4 us (2%)
  starting transfers between devices  18.9 us (1%)
    unnamed x8, waiting for transfers between devices  983 us
    unnamed x5, blocking collectives  229 us
    psum x2, blocking collectives, squared(): return lax.psum(local_inner(residual, precond), ('stu', 'que'))  193 us
    psum x1, blocking collectives, shards(): alpha = norm_now / lax.psum(local_inner(direction, image), ('stu', 'que'))  98.3 us
    all_gather x2, blocking collectives, shards(): va_cols = lax.all_gather(direction[1], 'stu', axis=0, tiled=True)  65.1 us
    all_gather x1, blocking collectives, shards(): theta_rows = lax.all_gather(theta, 'que', axis=0, tiled=True)  60 us
  transfers between devices with their start and end apart: 6, of which 4 were waited for; matrix products, arithmetic and copies ran while one was open for 0% of the time, Pallas kernels for 0%

profile of v1, /device:TPU:1, one launch (start us, length us, event | category | flops | bytes accessed | tf_op | source)
XLA Modules:
  0.0 1734.0 jit_solution(1418670617363818204)
XLA Ops:
  7.2 60.0 %all_gather.21 = f32[256,64]{1,0:T(8,128)S(1)} all-gather(f32[8,64]{1,0:T(8,128)} %param.5), channel_id=1, replica_groups=mesh['stu'=16,'que'=32] {'que'}, dimensions={0}, use_global_device_ids=true | all-gather | bytes 67584 | tf_op jit(solution)/shard_map/all_gather | solution.py:33
  67.2 0.7 copy-done.5
  67.9 0.6 fusion.47
  69.4 36.2 %all-reduce = f32[128]{0:T(128)S(1)} all-reduce(f32[128]{0:T(128)S(1)} %dynamic-update-slice), channel_id=1, replica_groups=mesh['stu'=16,'que'=32] {'stu'}, use_global_device_ids=true, to_apply=%add | all-reduce | flops 128 | bytes 1024
  105.6 30.4 %all_gather.22 = f32[128,64]{1,0:T(8,128)S(1)} all-gather(f32[8,64]{1,0:T(8,128)S(1)} %copy-done.2), channel_id=1, replica_groups=mesh['stu'=16,'que'=32] {'stu'}, dimensions={0}, use_global_device_ids=true | all-gather | bytes 34816 | tf_op jit(solution)/shard_map/all_gather | solution.py:35
  136.4 0.9 fusion.38
  137.3 0.9 fusion.18
  138.3 1.0 fusion.37
  139.3 1.0 fusion.10
  140.3 32.7 %all-reduce.20 = (f32[128]{0:T(128)S(1)}, f32[128]{0:T(128)S(1)}) all-reduce(f32[128]{0:T(128)S(1)} %get-tuple-element.35, f32[128]{0:T(128)S(1)} %get-tuple-element.31), channel_id=6, replica_groups=mesh['stu'=16,'que'=32] {'stu'}, use_global_device_ids=true, to_apply=%region_7.0.clone | all-reduce | flops 256 | bytes 2048
  174.4 1.3 dynamic-slice.3
  176.3 308.9 %all-reduce.30.cloned.1.call-done = (f32[256,64]{1,0:T(8,128)}, f32[256,64]{1,0:T(8,128)}) async-done(((f32[256,64]{1,0:T(8,128)}, f32[256,64]{1,0:T(8,128)}), (f32[256,64]{1,0:T(8,128)}, f32[256,64]{1,0:T(8,128)})) %all-reduce.30.cloned.1.call-update) | async-done | bytes 131088
  485.2 0.7 fusion.27
  485.9 0.7 reshape.48
  486.7 9.8 all-to-all-start
  496.6 137.9 %all-reduce.32.cloned.1.call-done = (f32[128,64]{1,0:T(8,128)}, f32[128,64]{1,0:T(8,128)}, f32[128]{0:T(128)}) async-done(((f32[128,64]{1,0:T(8,128)}, f32[128,64]{1,0:T(8,128)}, f32[128]{0:T(128)}), (f32[128,64]{1,0:T(8,128)}, f32[128,64]{1,0:T(8,128)}, f32[128]{0:T(128)})) %all-reduce.32.cloned.1.call-update) | async-done | bytes 66064
  634.4 0.7 fusion.29
  635.1 35.0 %all_gather.24 = f32[128,64]{1,0:T(8,128)S(1)} all-gather(f32[8,64]{1,0:T(8,128)S(1)} %get-tuple-element.26), channel_id=1, replica_groups=mesh['stu'=16,'que'=32] {'stu'}, dimensions={0}, use_global_device_ids=true | all-gather | bytes 34816 | tf_op jit(solution)/shard_map/all_gather | solution.py:72
  670.1 0.5 broadcast.60
  670.7 0.8 reduce
  671.6 0.7 copy-done.3
  672.6 0.9 fusion.50
  673.9 62.3 %all-reduce.18 = (f32[128,64]{1,0:T(8,128)S(1)}, f32[128]{0:T(128)S(1)}) all-reduce(f32[128,64]{1,0:T(8,128)S(1)} %fusion.51, f32[128]{0:T(128)S(1)} %get-tuple-element.39), channel_id=9, replica_groups=mesh['stu'=16,'que'=32] {'stu'}, use_global_device_ids=true, to_apply=%region_14.0.clone | all-reduce | flops 8320 | bytes 66560
  736.2 0.7 multiply_reduce_fusion.2
  736.9 0.7 multiply_reduce_fusion.7
  737.6 268.9 %all-reduce.26.cloned.1.call-done = f32[256,64]{1,0:T(8,128)} async-done(((f32[256,64]{1,0:T(8,128)}), f32[256,64]{1,0:T(8,128)}) %all-reduce.26.cloned.1.call-update) | async-done | bytes 65552
  1006.4 1.4 multiply_reduce_fusion.3
  1011.6 98.3 %all-reduce.15 = (f32[]{:T(128)}, f32[]{:T(128)}) all-reduce(f32[]{:T(128)S(6)} %add.156, f32[]{:T(128)S(6)} %add.163), channel_id=1, replica_groups=mesh['stu'=16,'que'=32] {'stu','que'}, use_global_device_ids=true, to_apply=%region_11.0 | all-reduce | flops 2 | bytes 16 | tf_op jit(solution)/shard_map/psum | solution.py:25
  1111.2 1.3 multiply_reduce_fusion
  1112.6 0.7 multiply_reduce_fusion.6
  1113.3 1.3 multiply_reduce_fusion.1
  1116.4 94.4 %psum.30 = f32[]{:T(128)} all-reduce(f32[]{:T(128)S(6)} %add.168), channel_id=1, replica_groups=mesh['stu'=16,'que'=32] {'stu','que'}, use_global_device_ids=true, to_apply=%region_23.0 | all-reduce | flops 1 | bytes 8 | tf_op jit(solution)/shard_map/psum | solution.py:25
  1212.1 0.7 multiply_add_fusion
  1212.8 0.7 multiply_add_fusion.1
  1213.5 0.7 reshape.50
  1214.2 8.9 all-to-all-start.1
  1223.3 33.4 %all-reduce.2 = f32[128]{0:T(128)S(1)} all-reduce(f32[128]{0:T(128)S(1)} %get-tuple-element.22), channel_id=1, replica_groups=mesh['stu'=16,'que'=32] {'stu'}, use_global_device_ids=true, to_apply=%add.2 | all-reduce | flops 128 | bytes 1024
  1256.7 30.1 %all_gather.26 = f32[128,64]{1,0:T(8,128)S(1)} all-gather(f32[8,64]{1,0:T(8,128)S(1)} %multiply_add_fusion), channel_id=1, replica_groups=mesh['stu'=16,'que'=32] {'stu'}, dimensions={0}, use_global_device_ids=true | all-gather | bytes 34816 | tf_op jit(solution)/shard_map/all_gather | solution.py:72
  1286.8 0.8 reduce.1
  1288.1 0.9 fusion.52
  1289.4 64.4 %all-reduce.17 = (f32[128,64]{1,0:T(8,128)S(1)}, f32[128]{0:T(128)S(1)}) all-reduce(f32[128,64]{1,0:T(8,128)S(1)} %fusion.53, f32[128]{0:T(128)S(1)} %get-tuple-element.41), channel_id=12, replica_groups=mesh['stu'=16,'que'=32] {'stu'}, use_global_device_ids=true, to_apply=%region_26.0.clone | all-reduce | flops 8320 | bytes 66560
  1353.8 0.6 fusion.23
  1354.4 0.7 fusion.30
  1355.1 267.6 %all-reduce.28.cloned.1.call-done = f32[256,64]{1,0:T(8,128)} async-done(((f32[256,64]{1,0:T(8,128)}), f32[256,64]{1,0:T(8,128)}) %all-reduce.28.cloned.1.call-update) | async-done | bytes 65552
  1622.7 1.3 fusion.22
  1625.9 98.3 %psum.31 = f32[]{:T(128)} all-reduce(f32[]{:T(128)S(6)} %add.178), channel_id=1, replica_groups=mesh['stu'=16,'que'=32] {'stu','que'}, use_global_device_ids=true, to_apply=%region_31.0 | all-reduce | flops 1 | bytes 8 | tf_op jit(solution)/shard_map/psum | solution.py:85
  1725.5 1.3 sqrt_multiply_fusion
  1726.8 0.6 sqrt_multiply_fusion.2
  (37 shorter events, 3.3 us)
Async XLA Ops:
  7.2 128.9 %copy-start = (s32[256,128]{1,0:T(8,128)S(1)}, s32[256,128]{1,0:T(8,128)}, u32[]{:S(2)}) copy-start(s32[256,128]{1,0:T(8,128)} %param.4) | copy-start | bytes 393220
  7.2 478.1 %all-reduce.30.cloned.1.call-start = ((), (), s32[]{:S(2)}) async-start(), calls=%async_computation.4 | async-start | bytes 524288
  67.2 0.7 copy-start.5
  68.5 0.7 copy-start.6
  69.2 36.4 %copy-start.2 = (f32[8,64]{1,0:T(8,128)S(1)}, f32[8,64]{1,0:T(8,128)}, u32[]{:S(2)}) copy-start(f32[8,64]{1,0:T(8,128)} %param.6) | copy-start | bytes 6148
  138.2 496.2 %all-reduce.32.cloned.1.call-start = ((), (), s32[]{:S(2)}) async-start(), calls=%async_computation.5 | async-start | bytes 263168
  173.8 0.5 copy-start.4
  175.7 309.6 %copy-start.1 = (f32[8,64]{1,0:T(8,128)S(1)}, f32[8,64]{1,0:T(8,128)}, u32[]{:S(2)}) copy-start(f32[8,64]{1,0:T(8,128)} %param.5) | copy-start | bytes 6148
  486.7 183.4 %all-to-all-start = ((f32[32,1,512]{2,1,0:T(1,128)}), f32[32,1,512]{2,1,0:T(1,128)S(1)}, u32[]{:S(2)}, u32[]{:S(2)}) async-start(f32[32,1,512]{2,1,0:T(1,128)} %reshape.48), calls=%async_computation | async-start | bytes 131072 | tf_op jit(solution)/shard_map/all_to_all | solution.py:71
  496.5 509.9 %all-reduce.26.cloned.1.call-start = ((), (), s32[]{:S(2)}) async-start(), calls=%async_computation.2 | async-start | bytes 262144
  671.5 0.7 copy-start.3
  1214.2 72.6 %all-to-all-start.1 = ((f32[32,1,512]{2,1,0:T(1,128)}), f32[32,1,512]{2,1,0:T(1,128)S(1)}, u32[]{:S(2)}, u32[]{:S(2)}) async-start(f32[32,1,512]{2,1,0:T(1,128)} %reshape.50), calls=%async_computation.1 | async-start | bytes 131072 | tf_op jit(solution)/shard_map/all_to_all | solution.py:71
  1223.1 399.5 %all-reduce.28.cloned.1.call-start = ((), (), s32[]{:S(2)}) async-start(), calls=%async_computation.3 | async-start | bytes 262144
Sparse Core Ops, SparseCore 0:
  138.4 346.8 all-reduce.29
  488.9 145.4 all-reduce.31
  674.0 332.3 all-reduce.25
  1289.5 333.1 all-reduce.27
